TPU v7x, 32 devices: a whole 2x2x4 slice. The times are simulated.
32 devices in a mesh: dp: 8 (over z, y), tensor: 4 (over x, core).
Axes of the slice: x: 2, y: 2, z: 4, core: 2. Of those that a mesh axis runs over, the one named last changes fastest.
Arguments:
- hidden: bfloat16 [16384, 768], P('dp'), may hold values from -6 to 6
- cotangent: bfloat16 [16384, 768], P('dp'), may hold values from -6 to 6
- seg_ids: int32 [16384], P('dp'), may hold values from 0 to 1024, as said below
- counts: int32 [8], P('dp'), may hold values from 1024 to 2048, as said below
- norm_gain: float32 [768], replicated, may hold values from 0.5 to 1.5
- w_x: bfloat16 [768, 1536], P(None, 'tensor'), may hold values from -0.21875 to 0.21875
- w_z: bfloat16 [768, 1536], P(None, 'tensor'), may hold values from -0.21875 to 0.21875
- w_dt: bfloat16 [768, 24], P(None, 'tensor'), may hold values from -0.21875 to 0.21875
- w_bc: bfloat16 [768, 256], replicated, may hold values from -0.21875 to 0.21875
- conv_x: float32 [4, 1536], P(None, 'tensor'), may hold values from -3 to 3
- conv_x_bias: float32 [1536], P('tensor'), may hold values from -0.5 to 0.5
- conv_bc: float32 [4, 256], replicated, may hold values from -3 to 3
- conv_bc_bias: float32 [256], replicated, may hold values from -0.5 to 0.5
- dt_bias: float32 [24], P('tensor'), may hold values from -4 to -1
- a_log: float32 [24], P('tensor'), may hold values from -1 to 2.5
- d_skip: float32 [24], P('tensor'), may hold values from 0.5 to 1.5
- gate_gain: float32 [1536], P('tensor'), may hold values from 0.5 to 1.5
- w_out: bfloat16 [1536, 768], P('tensor'), may hold values from -0.15625 to 0.15625
Outputs:
- block_out: bfloat16 [16384, 768], P('dp')
- grad_hidden: float32 [16384, 768], P('dp')
- grad_norm_gain: float32 [768], replicated
- grad_w_x: float32 [768, 1536], P(None, 'tensor')
- grad_w_z: float32 [768, 1536], P(None, 'tensor')
- grad_w_dt: float32 [768, 24], P(None, 'tensor')
- grad_w_bc: float32 [768, 256], replicated
- grad_conv_x: float32 [4, 1536], P(None, 'tensor')
- grad_conv_x_bias: float32 [1536], P('tensor')
- grad_conv_bc: float32 [4, 256], replicated
- grad_conv_bc_bias: float32 [256], replicated
- grad_dt_bias: float32 [24], P('tensor')
- grad_a_log: float32 [24], P('tensor')
- grad_d_skip: float32 [24], P('tensor')
- grad_gate_gain: float32 [1536], P('tensor')
- grad_w_out: float32 [1536, 768], P('tensor')
Inputs may be any that keep to these rules, and one draw needn't show every extreme that they name: `seg_ids`: within each shard of 2048 slots the ids start at 0, never fall and rise by at most 1 from slot to slot; slots 0 to 1023 have id 0 and slot 1024 starts a new id; in some shard every slot from 1024 on starts a new id. `counts`: each shard's count is at least 1024; some shard is full in every draw.
All inputs are finite; a program needn't handle non-finite values.
Results may differ from a plain program's by a relative error of at most 0.012.
Values sent between devices are 32-bit elements; how exact they have to be, the bound alone decides.
No kernel may reach another device: no remote copies, remote signals or barrier semaphores. Data moves between devices by JAX's collectives and lax.ppermute only.
A program may use at most 128 MiB of HBM per device.

v0:
```python
import jax
import jax.numpy as jnp
from jax import lax
from jax.sharding import PartitionSpec as P

INNER = 1536
SPAN = 256
EPS = 1e-05


def silu_grad(values):
    sigmoid_of = jax.nn.sigmoid(values)
    return sigmoid_of * (1.0 + values * (1.0 - sigmoid_of))


def lagged(values, offset):
    if offset == 0:
        return values
    padding = jnp.zeros((offset,) + values.shape[1:], values.dtype)
    return jnp.concatenate([padding, values[:-offset]], 0)


def leading(values, offset):
    padding = jnp.zeros((offset,) + values.shape[1:], values.dtype)
    return jnp.concatenate([values[offset:], padding], 0)


def conv_apply(values, weight, bias, conv_masks):
    total = bias + weight[0] * values
    for offset in range(1, len(conv_masks)):
        total = total + weight[offset] * lagged(values, offset) * conv_masks[offset]
    return total


def conv_back(values, weight, conv_masks, grad_pre):
    grad_weight = jnp.stack(
        [
            jnp.sum(grad_pre * conv_masks[offset] * lagged(values, offset), 0)
            for offset in range(len(conv_masks))
        ],
        0,
    )
    grad_bias = jnp.sum(grad_pre, 0)
    grad_values = grad_pre * weight[0]
    for offset in range(1, len(conv_masks)):
        grad_values = grad_values + leading(grad_pre * conv_masks[offset], offset) * weight[offset]
    return (grad_weight, grad_bias, grad_values)


def per_device(
    hidden,
    cotangent,
    seg_ids,
    counts,
    norm_gain,
    w_x,
    w_z,
    w_dt,
    w_bc,
    conv_x,
    conv_x_bias,
    conv_bc,
    conv_bc_bias,
    dt_bias,
    a_log,
    d_skip,
    gate_gain,
    w_out,
):
    row_count = hidden.shape[0]
    state_width = w_bc.shape[1] // 2
    heads_here = w_dt.shape[1]
    width_here = w_x.shape[1]
    head_size = width_here // heads_here
    tap_count = conv_x.shape[0]
    span_count = row_count // SPAN
    highest = lax.Precision.HIGHEST
    positions = jnp.arange(row_count)
    live_rows = (positions < counts[0]).astype(jnp.float32)[:, None]
    conv_masks = [
        ((lagged(seg_ids, offset) == seg_ids) & (positions >= offset)).astype(jnp.float32)[:, None]
        for offset in range(tap_count)
    ]
    hidden_wide = hidden.astype(jnp.float32)
    inv_rms = lax.rsqrt(jnp.mean(hidden_wide * hidden_wide, -1, keepdims=True) + EPS)
    normed = (hidden_wide * inv_rms * norm_gain).astype(jnp.bfloat16)
    normed_wide = normed.astype(jnp.float32)
    proj_x = jnp.dot(normed, w_x, preferred_element_type=jnp.float32)
    proj_z = jnp.dot(normed, w_z, preferred_element_type=jnp.float32)
    proj_dt = jnp.dot(normed, w_dt, preferred_element_type=jnp.float32)
    proj_bc = jnp.dot(normed, w_bc, preferred_element_type=jnp.float32)
    x_pre = conv_apply(proj_x, conv_x, conv_x_bias, conv_masks)
    bc_pre = conv_apply(proj_bc, conv_bc, conv_bc_bias, conv_masks)
    x_conv = jax.nn.silu(x_pre)
    bc_conv = jax.nn.silu(bc_pre)
    b_low = bc_conv[:, :state_width].astype(jnp.bfloat16)
    c_low = bc_conv[:, state_width:].astype(jnp.bfloat16)
    dt_in = proj_dt + dt_bias
    step_size = jax.nn.softplus(dt_in)
    rates = -jnp.exp(a_log)
    log_decay = jnp.cumsum(step_size * rates, 0)
    x_heads = x_conv.reshape(row_count, heads_here, head_size)
    inputs = (step_size[:, :, None] * x_heads).astype(jnp.bfloat16)
    ld_blocks = log_decay.reshape(span_count, SPAN, heads_here)
    seg_blocks = seg_ids.reshape(span_count, SPAN)
    local_pos = jnp.arange(SPAN)
    intra = (local_pos[:, None] >= local_pos[None, :])[None] & (
        seg_blocks[:, :, None] == seg_blocks[:, None, :]
    )
    ld_heads = jnp.transpose(ld_blocks, (0, 2, 1))
    exponent = jnp.where(
        intra[:, None], ld_heads[:, :, :, None] - ld_heads[:, :, None, :], -10000.0
    )
    decays = jnp.exp(exponent)
    b_blocks = b_low.reshape(span_count, SPAN, state_width)
    c_blocks = c_low.reshape(span_count, SPAN, state_width)
    inputs_blocks = inputs.reshape(span_count, SPAN, heads_here, head_size)
    kernel = jnp.einsum("cpn,cqn->cpq", c_blocks, b_blocks, preferred_element_type=jnp.float32)
    mixing = (kernel[:, None] * decays).astype(jnp.bfloat16)
    local_part = jnp.einsum(
        "chpq,cqhd->cphd", mixing, inputs_blocks, preferred_element_type=jnp.float32
    )
    ld_end = ld_blocks[:, -1]
    seg_end = seg_blocks[:, -1]
    in_keep = (seg_blocks == seg_end[:, None])[:, :, None]
    decay_in = jnp.where(in_keep, jnp.exp(ld_end[:, None, :] - ld_blocks), 0.0)
    b_blocks_wide = b_blocks.astype(jnp.float32)
    weighted_b = (b_blocks_wide[:, :, None, :] * decay_in[..., None]).astype(jnp.bfloat16)
    span_new = jnp.einsum(
        "cqhn,cqhd->chnd", weighted_b, inputs_blocks, preferred_element_type=jnp.float32
    )
    hop = jnp.where((seg_end[1:] == seg_end[:-1])[:, None], jnp.exp(ld_end[1:] - ld_end[:-1]), 0.0)
    state = jnp.zeros((heads_here, state_width, head_size), jnp.float32)
    befores = []
    for span in range(span_count):
        befores.append(state)
        if span == 0:
            state = span_new[0]
        else:
            state = hop[span - 1][:, None, None] * state + span_new[span]
    states_before = jnp.stack(befores, 0)
    carried_low = states_before.astype(jnp.bfloat16)
    prev_seg = jnp.concatenate([jnp.full((1,), -1, jnp.int32), seg_end[:-1]], 0)
    prev_ld = jnp.concatenate([jnp.zeros((1, heads_here), jnp.float32), ld_end[:-1]], 0)
    out_keep = (seg_blocks == prev_seg[:, None])[:, :, None]
    decay_out = jnp.where(out_keep, jnp.exp(ld_blocks - prev_ld[:, None, :]), 0.0)
    cross_raw = jnp.einsum(
        "cpn,chnd->cphd", c_blocks, carried_low, preferred_element_type=jnp.float32
    )
    scanned = (local_part + decay_out[..., None] * cross_raw).reshape(
        row_count, heads_here, head_size
    )
    y_flat = (scanned + d_skip[None, :, None] * x_heads).reshape(row_count, width_here)
    z_active = jax.nn.silu(proj_z)
    gated_out = y_flat * z_active
    squares = lax.psum(jnp.sum(gated_out * gated_out, -1), "tensor")
    inv_gate = lax.rsqrt(squares[:, None] / INNER + EPS)
    scaled = gated_out * inv_gate
    out_in = (scaled * gate_gain).astype(jnp.bfloat16)
    mixed = lax.psum(jnp.dot(out_in, w_out, preferred_element_type=jnp.float32), "tensor")
    output = (hidden_wide + live_rows * mixed).astype(jnp.bfloat16)
    grad_out = cotangent.astype(jnp.float32)
    grad_mix = (live_rows * grad_out).astype(jnp.bfloat16)
    grad_w_out = jnp.dot(out_in.T, grad_mix, preferred_element_type=jnp.float32)
    grad_in = jnp.dot(grad_mix, w_out.T, preferred_element_type=jnp.float32)
    grad_gate_gain = jnp.sum(grad_in * scaled, 0)
    grad_scaled = grad_in * gate_gain
    cross_sum = lax.psum(jnp.sum(grad_scaled * gated_out, -1), "tensor")
    grad_gated = inv_gate * grad_scaled - gated_out * inv_gate**3 * cross_sum[:, None] / INNER
    grad_y = (grad_gated * z_active).reshape(row_count, heads_here, head_size)
    grad_z = (grad_gated * y_flat * silu_grad(proj_z)).astype(jnp.bfloat16)
    grad_d_skip = jnp.sum(grad_y * x_heads, (0, 2))
    grad_scan = grad_y.astype(jnp.bfloat16)
    grad_scan_blocks = grad_scan.reshape(span_count, SPAN, heads_here, head_size)
    grad_mixing = jnp.einsum(
        "cphd,cqhd->chpq", grad_scan_blocks, inputs_blocks, preferred_element_type=jnp.float32
    )
    grad_inputs_blocks = jnp.einsum(
        "chpq,cphd->cqhd", mixing, grad_scan_blocks, preferred_element_type=jnp.float32
    )
    grad_kernel = (grad_mixing * decays).astype(jnp.bfloat16)
    grad_expo = grad_mixing * kernel[:, None] * decays
    grad_ld = jnp.transpose(jnp.sum(grad_expo, 3) - jnp.sum(grad_expo, 2), (0, 2, 1))
    grad_c_blocks = jnp.einsum(
        "chpq,cqn->cpn", grad_kernel, b_blocks, preferred_element_type=jnp.float32
    )
    grad_b_blocks = jnp.einsum(
        "chpq,cpn->cqn", grad_kernel, c_blocks, preferred_element_type=jnp.float32
    )
    grad_scan_wide = grad_scan_blocks.astype(jnp.float32)
    grad_decay_out = jnp.sum(grad_scan_wide * cross_raw, -1)
    grad_cross_raw = decay_out[..., None] * grad_scan_wide
    grad_c_blocks = grad_c_blocks + jnp.einsum(
        "cphd,chnd->cpn",
        grad_cross_raw,
        carried_low.astype(jnp.float32),
        precision=highest,
        preferred_element_type=jnp.float32,
    )
    grad_states = jnp.einsum(
        "cpn,cphd->chnd",
        c_blocks.astype(jnp.float32),
        grad_cross_raw,
        precision=highest,
        preferred_element_type=jnp.float32,
    )
    out_term = grad_decay_out * decay_out
    grad_ld = grad_ld + out_term
    grad_prev_ld = -jnp.sum(out_term, 1)
    grad_end = jnp.concatenate([grad_prev_ld[1:], jnp.zeros((1, heads_here), jnp.float32)], 0)
    flow = jnp.zeros((heads_here, state_width, head_size), jnp.float32)
    grad_new_list = [flow] * span_count
    hop_grads = []
    for span in reversed(range(span_count)):
        grad_new_list[span] = flow
        if span > 0:
            hop_grads.append(jnp.sum(flow * states_before[span], (1, 2)))
            flow = grad_states[span] + hop[span - 1][:, None, None] * flow
    grad_new = jnp.stack(grad_new_list, 0)
    hop_terms = jnp.stack(hop_grads[::-1], 0) * hop
    zero_row = jnp.zeros((1, heads_here), jnp.float32)
    grad_end = (
        grad_end
        + jnp.concatenate([zero_row, hop_terms], 0)
        - jnp.concatenate([hop_terms, zero_row], 0)
    )
    grad_weighted_b = jnp.einsum(
        "chnd,cqhd->cqhn",
        grad_new,
        inputs_blocks.astype(jnp.float32),
        precision=highest,
        preferred_element_type=jnp.float32,
    )
    grad_inputs_blocks = grad_inputs_blocks + jnp.einsum(
        "chnd,cqhn->cqhd",
        grad_new,
        weighted_b.astype(jnp.float32),
        precision=highest,
        preferred_element_type=jnp.float32,
    )
    grad_b_blocks = grad_b_blocks + jnp.sum(grad_weighted_b * decay_in[..., None], 2)
    in_term = jnp.sum(grad_weighted_b * b_blocks_wide[:, :, None, :], -1) * decay_in
    grad_end = grad_end + jnp.sum(in_term, 1)
    grad_ld = grad_ld - in_term
    end_mask = (local_pos == SPAN - 1).astype(jnp.float32)[None, :, None]
    grad_ld = grad_ld + end_mask * grad_end[:, None, :]
    grad_log = grad_ld.reshape(row_count, heads_here)
    grad_rate_sum = jnp.cumsum(grad_log[::-1], 0)[::-1]
    grad_inputs = grad_inputs_blocks.reshape(row_count, heads_here, head_size)
    grad_step = jnp.sum(grad_inputs * x_heads, -1) + grad_rate_sum * rates
    grad_a_log = jnp.sum(grad_rate_sum * step_size, 0) * rates
    grad_dt_in = grad_step * jax.nn.sigmoid(dt_in)
    grad_dt_bias = jnp.sum(grad_dt_in, 0)
    grad_x_heads = grad_y * d_skip[None, :, None] + grad_inputs * step_size[:, :, None]
    grad_bc = jnp.concatenate(
        [
            grad_b_blocks.reshape(row_count, state_width),
            grad_c_blocks.reshape(row_count, state_width),
        ],
        1,
    )
    grad_x_pre = grad_x_heads.reshape(row_count, width_here) * silu_grad(x_pre)
    grad_conv_x, grad_conv_x_bias, grad_proj_x = conv_back(proj_x, conv_x, conv_masks, grad_x_pre)
    grad_proj_low = grad_proj_x.astype(jnp.bfloat16)
    grad_w_x = jnp.dot(normed.T, grad_proj_low, preferred_element_type=jnp.float32)
    grad_w_z = jnp.dot(normed.T, grad_z, preferred_element_type=jnp.float32)
    grad_w_dt = jnp.dot(
        normed_wide.T, grad_dt_in, precision=highest, preferred_element_type=jnp.float32
    )
    partial_in = (
        jnp.dot(grad_proj_low, w_x.T, preferred_element_type=jnp.float32)
        + jnp.dot(grad_z, w_z.T, preferred_element_type=jnp.float32)
        + jnp.dot(
            grad_dt_in,
            w_dt.astype(jnp.float32).T,
            precision=highest,
            preferred_element_type=jnp.float32,
        )
    )
    bc_total = lax.psum(grad_bc, "tensor")
    grad_bc_pre = bc_total * silu_grad(bc_pre)
    grad_conv_bc, grad_conv_bc_bias, grad_proj_bc = conv_back(
        proj_bc, conv_bc, conv_masks, grad_bc_pre
    )
    grad_w_bc = jnp.dot(
        normed_wide.T, grad_proj_bc, precision=highest, preferred_element_type=jnp.float32
    )
    from_state = jnp.dot(
        grad_proj_bc,
        w_bc.astype(jnp.float32).T,
        precision=highest,
        preferred_element_type=jnp.float32,
    )
    summed_in = lax.psum(partial_in, "tensor")
    grad_normed = summed_in + from_state
    weighted = grad_normed * norm_gain
    grad_norm_gain = jnp.sum(grad_normed * hidden_wide * inv_rms, 0)
    grad_hidden = (
        grad_out
        + inv_rms * weighted
        - hidden_wide * inv_rms**3 * jnp.mean(weighted * hidden_wide, -1, keepdims=True)
    )
    main_sums = lax.psum(
        (
            grad_norm_gain,
            grad_w_x,
            grad_w_z,
            grad_w_dt,
            grad_conv_x,
            grad_conv_x_bias,
            grad_dt_bias,
            grad_a_log,
            grad_d_skip,
            grad_gate_gain,
            grad_w_out,
        ),
        "dp",
    )
    state_sums = lax.psum((grad_w_bc, grad_conv_bc, grad_conv_bc_bias), "dp")
    return (
        output,
        grad_hidden,
        main_sums[0],
        main_sums[1],
        main_sums[2],
        main_sums[3],
        state_sums[0],
        main_sums[4],
        main_sums[5],
        state_sums[1],
        state_sums[2],
        main_sums[6],
        main_sums[7],
        main_sums[8],
        main_sums[9],
        main_sums[10],
    )


def solution(mesh):
    return jax.shard_map(
        per_device,
        mesh=mesh,
        in_specs=(
            P("dp", None),
            P("dp", None),
            P("dp"),
            P("dp"),
            P(),
            P(None, "tensor"),
            P(None, "tensor"),
            P(None, "tensor"),
            P(),
            P(None, "tensor"),
            P("tensor"),
            P(),
            P(),
            P("tensor"),
            P("tensor"),
            P("tensor"),
            P("tensor"),
            P("tensor", None),
        ),
        out_specs=(
            P("dp", None),
            P("dp", None),
            P(),
            P(None, "tensor"),
            P(None, "tensor"),
            P(None, "tensor"),
            P(),
            P(None, "tensor"),
            P("tensor"),
            P(),
            P(),
            P("tensor"),
            P("tensor"),
            P("tensor"),
            P("tensor"),
            P("tensor", None),
        ),
        check_vma=False,
    )
```

profile of v0, /device:TPU:0, one launch (start us, length us, event | category | flops | bytes accessed | tf_op | source)
XLA Modules:
  0.0 647.3 jit_solution(8219857742431929211)
XLA Ops:
  7.3 2.7 fusion.6
  14.8 2.0 reduce-window.14
  20.3 3.7 fusion.94
  24.3 4.9 fusion.37
  29.2 3.6 copy.189
  32.7 5.2 copy.238
  39.1 3.4 multiply_convert_fusion.10
  43.5 2.2 copy.195
  53.5 5.2 bitcast_add_fusion.1
  60.6 3.1 copy.242
  63.6 3.5 copy.204
  67.3 9.4 %multiply_reduce_fusion.7 = (f32[2048]{0:T(1024)S(1)}, f32[2048,384]{1,0:T(8,128)}, f32[2048,384]{1,0:T(8,128)}) fusion(f32[2048,384]{1,0:T(8,128)} %copy.204, f32[2048,384]{1,0:T(8,128)} %get-tuple-element.98, f32[384]{0:T(512)S(1)} %mul.880, bf16[2048,768]{1,0:T(8,128)(2,1)} %copy-done.3, bf16[768,384]{1,0:T(8,128)(2,1)S(1)} %copy-done), kind=kOutput, calls=%fused_computation.67 | convolution fusion | flops 1218181120 | bytes 16328192 | tf_op jit(solution)/shard_map/dot_general | solution.py:89
  76.7 8.5 %psum.133 = f32[2048]{0:T(1024)S(1)} all-reduce(f32[2048]{0:T(1024)S(1)} %get-tuple-element.89), channel_id=1, replica_groups=mesh['dp'=8,'tensor'=4] {'tensor'}, use_global_device_ids=true, to_apply=%region_4.5 | all-reduce | flops 2048 | bytes 16384 | tf_op jit(solution)/shard_map/psum | solution.py:156
  85.9 7.4 %multiply_reduce_fusion = (f32[384]{0:T(512)}, f32[2048]{0:T(1024)S(1)}, f32[2048,384]{1,0:T(8,128)}) fusion(f32[2048,384]{1,0:T(8,128)} %get-tuple-element.90, f32[2048]{0:T(1024)S(1)} %get-tuple-element.122, f32[384]{0:T(512)S(1)} %copy-done.70, bf16[384,768]{1,0:T(8,128)(2,1)} %param.35, bf16[2048,768]{1,0:T(8,128)(2,1)} %param.19, f32[2048]{0:T(1024)S(1)} %fusion.72), kind=kOutput, calls=%fused_computation.55 | convolution fusion | flops 1217394304 | bytes 10054656 | tf_op jit(solution)/shard_map/dot_general | solution.py:165
  93.3 5.8 psum.135
  99.2 9.2 %multiply_reduce_fusion.1 = (f32[384]{0:T(512)}, f32[2048,384]{1,0:T(8,128)S(1)}, bf16[2048,384]{1,0:T(8,128)(2,1)}) fusion(f32[2048,384]{1,0:T(8,128)} %get-tuple-element.98, f32[2048,384]{1,0:T(8,128)} %get-tuple-element.136, f32[2048]{0:T(1024)S(1)} %psum.135, f32[2048,384]{1,0:T(8,128)} %get-tuple-element.90, f32[2048]{0:T(1024)S(1)} %get-tuple-element.121, ...), kind=kLoop, calls=%fused_computation.56 | loop fusion | flops 20446848 | bytes 20476416 | tf_op jit(solution)/shard_map/reduce_sum | solution.py:172
  111.3 2.6 copy.205
  113.9 2.0 copy.243
  116.1 9.8 %fusion = (f32[8,6,256]{2,1,0:T(8,128)}, f32[8,6,256]{2,1,0:T(8,128)}, bf16[8,256,256]{2,1,0:T(8,128)(2,1)}) fusion(f32[8,6,256]{2,1,0:T(8,128)S(1)} %copy.190, f32[8,256,256]{2,1,0:T(8,128)S(1)} %copy-done.31, pred[8,256,256]{2,1,0:T(8,128)(4,1)S(1)} %copy-done.55, bf16[8,256,6,64]{1,0,3,2:T(8,128)(2,1)} %copy-done.34, ...), kind=kOutput, calls=%fused_computation.11 | convolution fusion | flops 433561600 | bytes 6963200 | tf_op jit(solution)/shard_map/cphd,cqhd->chpq/dot_general | solution.py:175
  125.9 3.7 fusion.42
  135.1 4.8 fusion.2
  140.0 4.5 fusion.85
  144.9 4.7 fusion.15
  149.6 2.6 copy.227
  152.2 3.2 convolution_add_fusion.3
  163.7 6.3 fusion.31
  171.8 3.1 copy.244
  174.9 3.6 copy.210
  178.5 2.0 mul.911
  180.6 3.6 copy.211
  184.2 6.5 %fusion.86 = (f32[384]{0:T(512)S(1)}, f32[384]{0:T(512)S(1)}, f32[2048,384]{1,0:T(8,128)S(1)}) fusion(f32[2048,384]{1,0:T(8,128)} %copy-done.1, f32[2048,384]{1,0:T(8,128)} %get-tuple-element.98, f32[2048,384]{1,0:T(8,128)} %copy.210, f32[2048,384]{1,0:T(8,128)} %copy.211, f32[2048,384]{1,0:T(8,128)} %copy-done.12, f32[384]{0:T(512)S(1)} %copy-done.101), kind=kLoop, calls=%fused_computation.247 | loop fusion | flops 11009280 | bytes 18878976 | tf_op jit(solution)/shard_map/reduce_sum | solution.py:43
  190.7 2.8 multiply_reduce_fusion.4
  195.7 1.8 fusion.98
  197.7 1.8 fusion.99
  201.3 4.7 add_add_fusion
  206.1 5.3 fusion.100
  211.4 2.8 fusion.101
  214.3 2.8 fusion.43
  217.1 244.0 %all-reduce.26.cloned.1.call-done = (f32[2048,768]{1,0:T(8,128)}, f32[2048,768]{1,0:T(8,128)}, f32[2048,256]{1,0:T(8,128)}) async-done(((f32[2048,768]{1,0:T(8,128)}, f32[2048,768]{1,0:T(8,128)}, f32[2048,256]{1,0:T(8,128)}), (f32[2048,768]{1,0:T(8,128)}, f32[2048,768]{1,0:T(8,128)}, f32[2048,256]{1,0:T(8,128)})) %all-reduce.26.cloned.1.call-update) | async-done | bytes 14680080 | tf_op jit(solution)/shard_map/psum | solution.py:160
  461.2 3.1 fusion.87
  464.3 2.1 multiply_reduce_fusion.10
  469.3 4.5 fusion.103
  474.7 3.3 fusion.102
  478.1 8.3 %fusion.13 = (f32[768]{0:T(1024)S(1)}, f32[2048]{0:T(1024)S(1)}, f32[2048,768]{1,0:T(8,128)}) fusion(bf16[2048,768]{1,0:T(8,128)(2,1)S(1)} %copy-done.8, f32[2048]{0:T(1024)S(1)} %copy-done.67, f32[768]{0:T(1024)S(1)} %copy-done.78, f32[2048,768]{1,0:T(8,128)} %get-tuple-element.61, f32[2048,256]{1,0:T(8,128)S(1)} %multiply_add_fusion.2, ...), kind=kOutput, calls=%fused_computation.26 | convolution fusion | flops 4844418048 | bytes 18241536 | tf_op jit(solution)/shard_map/dot_general | solution.py:288
  486.5 40.8 %all-reduce.18 = (f32[768]{0:T(1024)}, f32[768,6]{0,1:T(8,128)}, f32[4,384]{1,0:T(4,128)}, f32[384]{0:T(512)}, f32[4,256]{1,0:T(4,128)}, /*index=5*/f32[256]{0:T...) all-reduce(f32[768]{0:T(1024)S(1)} %get-tuple-element.19, ...), channel_id=1, replica_groups=mesh['dp'=8,'tensor'=4] {'dp'}, use_global_device_ids=true, to_apply=%region_30.31 | all-reduce | flops 8978 | bytes 71824 | tf_op jit(solution)/shard_map/psum | solution.py:303
  527.3 11.3 %fusion.5 = (f32[2048,768]{1,0:T(8,128)}, bf16[2048,768]{1,0:T(8,128)(2,1)}) fusion(bf16[2048,768]{1,0:T(8,128)(2,1)} %param.19, bf16[2048,768]{1,0:T(8,128)(2,1)} %param.18, f32[2048,768]{1,0:T(8,128)} %get-tuple-element.140, f32[2048]{0:T(1024)S(1)} %broadcast_multiply_fusion.6, f32[2048]{0:T(1024)S(1)} %copy-done.79, f32[768]{0:T(1024)S(1)} %copy-done.78, ...), kind=kLoop, calls=%fused_computation.18 | loop fusion | flops 17301504 | bytes 28347392 | tf_op jit(solution)/shard_map/sub | solution.py:299
  538.6 96.2 %all-reduce.24.cloned.1.call-done = (f32[768,384]{1,0:T(8,128)}, f32[768,384]{1,0:T(8,128)}, f32[768,256]{1,0:T(8,128)}, f32[384,768]{1,0:T(8,128)}) async-done(((f32[768,384]{1,0:T(8,128)}, f32[768,384]{1,0:T(8,128)}, f32[768,256]{1,0:T(8,128)}, f32[384,768]{1,0:T(8,128)}), (f32[768,384]{1,0:T(8,128)}, f32[768,384]{1,0:T(8,128)}, f32[768,256]{1,0:T(8,128)}, ...) | async-done | bytes 4325392 | tf_op jit(solution)/shard_map/psum | solution.py:303
  634.8 2.5 copy.314
  (385 shorter events, 49.4 us)
Async XLA Ops:
  7.2 60.1 %copy-start = (bf16[768,384]{1,0:T(8,128)(2,1)S(1)}, bf16[768,384]{1,0:T(8,128)(2,1)}, u32[]{:S(2)}) copy-start(bf16[768,384]{1,0:T(8,128)(2,1)} %param.24) | copy-start | bytes 1769476
  7.2 453.9 %all-reduce.26.cloned.1.call-start = ((), (), s32[]{:S(2)}) async-start(), calls=%async_computation.1 | async-start | bytes 29360128 | tf_op jit(solution)/shard_map/psum | solution.py:160
  13.7 6.6 %copy-start.52 = (bf16[768,384]{1,0:T(8,128)(2,1)S(1)}, bf16[768,384]{1,0:T(8,128)(2,1)}, u32[]{:S(2)}) copy-start(bf16[768,384]{1,0:T(8,128)(2,1)} %param.23) | copy-start | bytes 1769476
  14.6 9.4 %copy-start.46 = (f32[2048,6]{0,1:T(8,128)}, f32[2048,6]{0,1:T(8,128)S(1)}, u32[]{:S(2)}) copy-start(f32[2048,6]{0,1:T(8,128)S(1)} %get-tuple-element.135) | copy-start | bytes 147460
  14.7 23.3 %copy-start.44 = (f32[2048,6]{0,1:T(8,128)}, f32[2048,6]{0,1:T(8,128)S(1)}, u32[]{:S(2)}) copy-start(f32[2048,6]{0,1:T(8,128)S(1)} %get-tuple-element.134) | copy-start | bytes 147460
  24.1 5.1 copy-start.1
  24.1 5.0 copy-start.86
  24.1 5.0 copy-start.88
  24.1 5.0 copy-start.90
  24.1 5.0 copy-start.92
  24.2 14.8 %copy-start.58 = (f32[2048]{0:T(1024)}, f32[2048]{0:T(1024)S(1)}, u32[]{:S(2)}) copy-start(f32[2048]{0:T(1024)S(1)} %get-tuple-element.125) | copy-start | bytes 24580
  24.2 14.8 %copy-start.60 = (f32[2048]{0:T(1024)}, f32[2048]{0:T(1024)S(1)}, u32[]{:S(2)}) copy-start(f32[2048]{0:T(1024)S(1)} %get-tuple-element.126) | copy-start | bytes 24580
  24.3 14.8 %copy-start.62 = (f32[2048]{0:T(1024)}, f32[2048]{0:T(1024)S(1)}, u32[]{:S(2)}) copy-start(f32[2048]{0:T(1024)S(1)} %get-tuple-element.127) | copy-start | bytes 24580
  32.7 5.2 copy-start.4
  32.7 5.2 copy-start.36
  46.6 5.0 copy-start.115
  46.6 5.2 copy-start.80
  46.6 5.2 copy-start.97
  46.6 5.5 copy-start.83
  46.6 5.5 copy-start.94
  46.6 5.6 copy-start.104
  48.2 5.3 copy-start.30
  52.9 5.9 copy-start.19
  52.9 63.0 %copy-start.73 = (f32[8,6,256]{2,1,0:T(8,128)}, f32[8,6,256]{2,1,0:T(8,128)S(1)}, u32[]{:S(2)}) copy-start(f32[8,6,256]{2,1,0:T(8,128)S(1)} %copy.190) | copy-start | bytes 147460
  53.5 5.3 copy-start.54
  67.3 31.8 %copy-start.100 = (f32[384]{0:T(512)}, f32[384]{0:T(512)S(1)}, u32[]{:S(2)}) copy-start(f32[384]{0:T(512)S(1)} %mul.880) | copy-start | bytes 4612
  67.3 18.6 %copy-start.70 = (f32[384]{0:T(512)S(1)}, f32[384]{0:T(512)}, u32[]{:S(2)}) copy-start(f32[384]{0:T(512)} %param.34) | copy-start | bytes 4612
  85.9 7.4 %copy-start.68 = (f32[2048]{0:T(1024)}, f32[2048]{0:T(1024)S(1)}, u32[]{:S(2)}) copy-start(f32[2048]{0:T(1024)S(1)} %fusion.72) | copy-start | bytes 24580
  116.1 9.8 %copy-start.43 = (bf16[8,6,128,64]{2,3,1,0:T(8,128)(2,1)S(1)}, bf16[8,6,128,64]{2,3,1,0:T(8,128)(2,1)}, u32[]{:S(2)}) copy-start(bf16[8,6,128,64]{2,3,1,0:T(8,128)(2,1)} %copy-done.42) | copy-start | bytes 2359300
  125.9 5.6 copy-start.81
  125.9 5.6 copy-start.84
  125.9 5.6 copy-start.95
  125.9 5.6 copy-start.98
  125.9 5.6 copy-start.102
  125.9 5.6 copy-start.105
  125.9 5.6 copy-start.116
  131.4 13.3 %copy-start.16 = (f32[8,6,128,64]{2,3,1,0:T(8,128)}, f32[8,6,128,64]{2,3,1,0:T(8,128)S(1)}, u32[]{:S(2)}) copy-start(f32[8,6,128,64]{2,3,1,0:T(8,128)S(1)} %fusion.41) | copy-start | bytes 4718596
  139.9 4.9 copy-start.27
  184.1 6.5 %copy-start.2 = (f32[2048,384]{1,0:T(8,128)S(1)}, f32[2048,384]{1,0:T(8,128)}, u32[]{:S(2)}) copy-start(f32[2048,384]{1,0:T(8,128)} %copy-done.1) | copy-start | bytes 9437188
  184.1 6.5 %copy-start.59 = (f32[2048]{0:T(1024)S(1)}, f32[2048]{0:T(1024)}, u32[]{:S(2)}) copy-start(f32[2048]{0:T(1024)} %copy-done.58) | copy-start | bytes 24580
  184.1 6.5 %copy-start.61 = (f32[2048]{0:T(1024)S(1)}, f32[2048]{0:T(1024)}, u32[]{:S(2)}) copy-start(f32[2048]{0:T(1024)} %copy-done.60) | copy-start | bytes 24580
  184.2 6.5 %copy-start.63 = (f32[2048]{0:T(1024)S(1)}, f32[2048]{0:T(1024)}, u32[]{:S(2)}) copy-start(f32[2048]{0:T(1024)} %copy-done.62) | copy-start | bytes 24580
  206.0 428.8 %all-reduce.24.cloned.1.call-start = ((), (), s32[]{:S(2)}) async-start(), calls=%async_computation | async-start | bytes 8650752 | tf_op jit(solution)/shard_map/psum | solution.py:303
  206.1 5.4 copy-start.5
  206.1 5.4 copy-start.14
  206.1 8.2 %copy-start.18 = (bf16[2048,768]{1,0:T(8,128)(2,1)S(1)}, bf16[2048,768]{1,0:T(8,128)(2,1)}, u32[]{:S(2)}) copy-start(bf16[2048,768]{1,0:T(8,128)(2,1)} %param.19) | copy-start | bytes 9437188
  478.1 8.4 %copy-start.124 = (f32[384]{0:T(512)S(1)}, f32[384]{0:T(512)}, u32[]{:S(2)}) copy-start(f32[384]{0:T(512)} %get-tuple-element.21) | copy-start | bytes 4612
  478.1 49.2 %copy-start.79 = (f32[2048]{0:T(1024)S(1)}, f32[2048]{0:T(1024)}, u32[]{:S(2)}) copy-start(f32[2048]{0:T(1024)} %get-tuple-element.119) | copy-start | bytes 24580
  (85 other events, 226.7 us)
Sparse Core Ops, SparseCore 0:
  206.1 254.9 all-reduce.25
  473.9 160.7 all-reduce.23
where the time goes:
time: 650 us; the launch traced here: 647 us
  waiting for transfers between devices  340 us (52%)
  matrix products  107 us (16%)
  other arithmetic  64.3 us (10%)
  local copies, waits for them, and re-layouts  64 us (10%)
  blocking collectives  55.2 us (8%)
  between operations  16.7 us (3%)
    psum x1, waiting for transfers between devices, per_device(): lax.psum(jnp.dot(out_in, w_out, preferred_element_type=jnp.float32), 'ten...  244 us
    psum x1, waiting for transfers between devices, per_device(): lax.psum((grad_norm_gain, grad_w_x, grad_w_z, grad_w_dt, grad_conv_x, gra...  96.2 us
    psum x1, blocking collectives, per_device(): lax.psum((grad_norm_gain, grad_w_x, grad_w_z, grad_w_dt, grad_conv_x, gra...  40.8 us
    unnamed x284, local copies, waits for them, and re-layouts  29.5 us
  transfers between devices with their start and end apart: 2, of which 2 were waited for; matrix products, arithmetic and copies ran while one was open for 5% of the time, Pallas kernels for 0%

commit v1 on v0

--- a/solution.py
+++ b/solution.py
@@ -157,7 +157,9 @@
     inv_gate = lax.rsqrt(squares[:, None] / INNER + EPS)
     scaled = gated_out * inv_gate
     out_in = (scaled * gate_gain).astype(jnp.bfloat16)
-    mixed = lax.psum(jnp.dot(out_in, w_out, preferred_element_type=jnp.float32), "tensor")
+    block = jnp.dot(out_in, w_out, preferred_element_type=jnp.float32)
+    parts = lax.all_gather(block, "tensor", axis=0, tiled=False)
+    mixed = parts.sum(axis=0)
     output = (hidden_wide + live_rows * mixed).astype(jnp.bfloat16)
     grad_out = cotangent.astype(jnp.float32)
     grad_mix = (live_rows * grad_out).astype(jnp.bfloat16)

time: 650 us -> 691 us (1.063)
  waiting for transfers between devices: 340 us -> 368 us
  other arithmetic: 64.3 us -> 76.9 us
    psum x1, waiting for transfers between devices: 244 us -> 136 us  [per_device(): summed_in = lax.psum(partial_in, 'tensor')]
    all_gather x0 -> x1, waiting for transfers between devices: none -> 91.5 us  [per_device(): parts = lax.all_gather(block, 'tensor', axis=0, tiled=False)]
    psum x1, waiting for transfers between devices: 96.2 us -> 141 us  [per_device(): lax.psum((grad_norm_gain, grad_w_x, grad_w_z, grad_w_dt, grad_conv_x, gra...]
    reduce_sum x0 -> x1, other arithmetic: none -> 12.9 us  [per_device(): mixed = parts.sum(axis=0)]
    unnamed x284 -> x280, local copies, waits for them, and re-layouts: 29.5 us -> 30 us
  transfers between devices with their start and end apart: 2 -> 3, of which waited for: 2 -> 3; matrix products, arithmetic and copies ran while one was open for 5% -> 10% of each run, Pallas kernels for 0% -> 0%
where the time goes in v1:
time: 691 us; the launch traced here: 688 us
  waiting for transfers between devices  368 us (53%)
  matrix products  111 us (16%)
  other arithmetic  76.9 us (11%)
  local copies, waits for them, and re-layouts  64 us (9%)
  blocking collectives  52.4 us (8%)
  between operations  16.3 us (2%)
    psum x1, waiting for transfers between devices, per_device(): lax.psum((grad_norm_gain, grad_w_x, grad_w_z, grad_w_dt, grad_conv_x, gra...  141 us
    psum x1, waiting for transfers between devices, per_device(): summed_in = lax.psum(partial_in, 'tensor')  136 us
    all_gather x1, waiting for transfers between devices, per_device(): parts = lax.all_gather(block, 'tensor', axis=0, tiled=False)  91.5 us
    psum x1, blocking collectives, per_device(): lax.psum((grad_norm_gain, grad_w_x, grad_w_z, grad_w_dt, grad_conv_x, gra...  38.1 us
    unnamed x280, local copies, waits for them, and re-layouts  30 us
  transfers between devices with their start and end apart: 3, of which 3 were waited for; matrix products, arithmetic and copies ran while one was open for 10% of the time, Pallas kernels for 0%

profile of v1, /device:TPU:0, one launch (start us, length us, event | category | flops | bytes accessed | tf_op | source)
XLA Modules:
  0.0 688.0 jit_solution(16049821443330311347)
XLA Ops:
  7.3 2.7 fusion.6
  14.8 2.0 reduce-window.14
  20.3 3.7 fusion.94
  24.3 4.9 fusion.37
  29.2 3.6 copy.189
  32.8 5.2 copy.238
  39.1 3.4 multiply_convert_fusion.10
  43.4 2.2 copy.195
  53.5 5.2 bitcast_add_fusion.1
  60.5 3.1 copy.242
  63.6 3.6 copy.204
  67.4 9.2 %multiply_reduce_fusion.7 = (f32[2048]{0:T(1024)S(1)}, f32[2048,384]{1,0:T(8,128)}, f32[2048,384]{1,0:T(8,128)}) fusion(f32[2048,384]{1,0:T(8,128)} %copy.204, f32[2048,384]{1,0:T(8,128)} %get-tuple-element.97, f32[384]{0:T(512)S(1)} %mul.880, bf16[2048,768]{1,0:T(8,128)(2,1)} %copy-done.3, bf16[768,384]{1,0:T(8,128)(2,1)S(1)} %copy-done), kind=kOutput, calls=%fused_computation.67 | convolution fusion | flops 1218181120 | bytes 16328192 | tf_op jit(solution)/shard_map/dot_general | solution.py:89
  76.6 8.5 %psum.126 = f32[2048]{0:T(1024)S(1)} all-reduce(f32[2048]{0:T(1024)S(1)} %get-tuple-element.88), channel_id=1, replica_groups=mesh['dp'=8,'tensor'=4] {'tensor'}, use_global_device_ids=true, to_apply=%region_4.5 | all-reduce | flops 2048 | bytes 16384 | tf_op jit(solution)/shard_map/psum | solution.py:156
  85.8 7.4 %multiply_reduce_fusion = (f32[384]{0:T(512)}, f32[2048]{0:T(1024)S(1)}, f32[2048,384]{1,0:T(8,128)}) fusion(f32[2048,384]{1,0:T(8,128)} %get-tuple-element.89, f32[2048]{0:T(1024)S(1)} %get-tuple-element.121, f32[384]{0:T(512)S(1)} %copy-done.68, bf16[384,768]{1,0:T(8,128)(2,1)} %param.35, bf16[2048,768]{1,0:T(8,128)(2,1)} %param.19, f32[2048]{0:T(1024)S(1)} %fusion.72), kind=kOutput, calls=%fused_computation.55 | convolution fusion | flops 1217394304 | bytes 10054656 | tf_op jit(solution)/shard_map/dot_general | solution.py:167
  93.2 5.8 psum.127
  99.1 9.2 %multiply_reduce_fusion.1 = (f32[384]{0:T(512)}, f32[2048,384]{1,0:T(8,128)S(1)}, bf16[2048,384]{1,0:T(8,128)(2,1)}) fusion(f32[2048,384]{1,0:T(8,128)} %get-tuple-element.97, f32[2048,384]{1,0:T(8,128)} %get-tuple-element.135, f32[2048]{0:T(1024)S(1)} %psum.127, f32[2048,384]{1,0:T(8,128)} %get-tuple-element.89, f32[2048]{0:T(1024)S(1)} %get-tuple-element.120, ...), kind=kLoop, calls=%fused_computation.56 | loop fusion | flops 20446848 | bytes 20476416 | tf_op jit(solution)/shard_map/reduce_sum | solution.py:174
  111.3 2.6 copy.205
  113.9 2.0 copy.243
  116.1 9.8 %fusion = (f32[8,6,256]{2,1,0:T(8,128)}, f32[8,6,256]{2,1,0:T(8,128)}, bf16[8,256,256]{2,1,0:T(8,128)(2,1)}) fusion(f32[8,6,256]{2,1,0:T(8,128)S(1)} %copy.190, f32[8,256,256]{2,1,0:T(8,128)S(1)} %copy-done.30, pred[8,256,256]{2,1,0:T(8,128)(4,1)S(1)} %copy-done.53, bf16[8,256,6,64]{1,0,3,2:T(8,128)(2,1)} %copy-done.33, ...), kind=kOutput, calls=%fused_computation.11 | convolution fusion | flops 433561600 | bytes 6963200 | tf_op jit(solution)/shard_map/cphd,cqhd->chpq/dot_general | solution.py:177
  125.9 3.7 fusion.42
  135.1 4.6 fusion.2
  140.2 5.3 fusion.15
  145.5 2.5 copy.227
  148.0 3.2 convolution_add_fusion.3
  159.1 6.3 fusion.31
  167.2 3.0 copy.244
  170.3 3.6 copy.210
  173.9 2.0 mul.911
  175.9 3.5 copy.211
  179.5 6.5 fusion.86
  186.0 2.8 multiply_reduce_fusion.4
  196.6 4.7 add_add_fusion
  201.3 6.7 fusion.85
  208.2 5.3 fusion.100
  213.5 2.8 fusion.101
  216.4 2.8 fusion.43
  219.2 135.5 %all-reduce.26.cloned.1.call-done = (f32[2048,768]{1,0:T(8,128)}, f32[2048,256]{1,0:T(8,128)}) async-done(((f32[2048,768]{1,0:T(8,128)}, f32[2048,256]{1,0:T(8,128)}), (f32[2048,768]{1,0:T(8,128)}, f32[2048,256]{1,0:T(8,128)})) %all-reduce.26.cloned.1.call-update) | async-done | bytes 8388624 | tf_op jit(solution)/shard_map/psum | solution.py:296
  354.7 3.1 fusion.87
  357.9 2.1 multiply_reduce_fusion.10
  363.3 4.5 fusion.103
  368.7 3.9 fusion.102
  372.8 8.9 %fusion.13 = (f32[768]{0:T(1024)S(1)}, f32[2048]{0:T(1024)S(1)}, f32[2048,768]{1,0:T(8,128)}) fusion(bf16[2048,768]{1,0:T(8,128)(2,1)S(1)} %copy-done.8, f32[2048]{0:T(1024)S(1)} %copy-done.65, f32[768]{0:T(1024)S(1)} %copy-done.76, f32[2048,768]{1,0:T(8,128)} %get-tuple-element.60, f32[2048,256]{1,0:T(8,128)S(1)} %multiply_add_fusion.2, ...), kind=kOutput, calls=%fused_computation.26 | convolution fusion | flops 4844418048 | bytes 18241536 | tf_op jit(solution)/shard_map/dot_general | solution.py:290
  381.7 38.1 %all-reduce.18 = (f32[768]{0:T(1024)}, f32[768,6]{0,1:T(8,128)}, f32[4,384]{1,0:T(4,128)}, f32[384]{0:T(512)}, f32[4,256]{1,0:T(4,128)}, /*index=5*/f32[256]{0:T...) all-reduce(f32[768]{0:T(1024)S(1)} %get-tuple-element.19, ...), channel_id=1, replica_groups=mesh['dp'=8,'tensor'=4] {'dp'}, use_global_device_ids=true, to_apply=%region_30.31 | all-reduce | flops 8978 | bytes 71824 | tf_op jit(solution)/shard_map/psum | solution.py:305
  419.8 91.5 %all-gather.3.cloned.1.call-done = f32[8192,768]{1,0:T(8,128)} async-done(((f32[2048,768]{1,0:T(8,128)}), f32[8192,768]{1,0:T(8,128)}) %all-gather.3.cloned.1.call-update) | async-done | bytes 25165840 | tf_op jit(solution)/shard_map/all_gather | solution.py:161
  511.3 12.9 %reduce_sum.339 = f32[2048,768]{1,0:T(8,128)} reduce(f32[4,2048,768]{2,1,0:T(8,128)} %bitcast.275, f32[]{:T(128)} %constant.14.clone.1), dimensions={0}, to_apply=%region_5.6 | reduce | flops 4718592 | bytes 31457284 | tf_op jit(solution)/shard_map/reduce_sum | solution.py:162
  524.2 11.0 %fusion.5 = (f32[2048,768]{1,0:T(8,128)}, bf16[2048,768]{1,0:T(8,128)(2,1)}) fusion(bf16[2048,768]{1,0:T(8,128)(2,1)} %param.19, bf16[2048,768]{1,0:T(8,128)(2,1)} %param.18, f32[2048,768]{1,0:T(8,128)} %get-tuple-element.139, f32[2048]{0:T(1024)S(1)} %broadcast_multiply_fusion.6, f32[2048]{0:T(1024)S(1)} %copy-done.77, f32[768]{0:T(1024)S(1)} %copy-done.76, ...), kind=kLoop, calls=%fused_computation.18 | loop fusion | flops 17301504 | bytes 28347392 | tf_op jit(solution)/shard_map/sub | solution.py:301
  535.2 140.7 %all-reduce.24.cloned.1.call-done = (f32[768,384]{1,0:T(8,128)}, f32[768,384]{1,0:T(8,128)}, f32[768,256]{1,0:T(8,128)}, f32[384,768]{1,0:T(8,128)}) async-done(((f32[768,384]{1,0:T(8,128)}, f32[768,384]{1,0:T(8,128)}, f32[768,256]{1,0:T(8,128)}, f32[384,768]{1,0:T(8,128)}), (f32[768,384]{1,0:T(8,128)}, f32[768,384]{1,0:T(8,128)}, f32[768,256]{1,0:T(8,128)}, ...) | async-done | bytes 4325392 | tf_op jit(solution)/shard_map/psum | solution.py:305
  675.9 2.5 copy.313
  (385 shorter events, 53.2 us)
Async XLA Ops:
  7.2 60.2 %copy-start = (bf16[768,384]{1,0:T(8,128)(2,1)S(1)}, bf16[768,384]{1,0:T(8,128)(2,1)}, u32[]{:S(2)}) copy-start(bf16[768,384]{1,0:T(8,128)(2,1)} %param.24) | copy-start | bytes 1769476
  7.2 347.5 %all-reduce.26.cloned.1.call-start = ((), (), s32[]{:S(2)}) async-start(), calls=%async_computation.2 | async-start | bytes 16777216 | tf_op jit(solution)/shard_map/psum | solution.py:296
  13.7 6.6 copy-start.50
  14.6 9.4 %copy-start.45 = (f32[2048,6]{0,1:T(8,128)}, f32[2048,6]{0,1:T(8,128)S(1)}, u32[]{:S(2)}) copy-start(f32[2048,6]{0,1:T(8,128)S(1)} %get-tuple-element.134) | copy-start | bytes 147460
  14.7 23.3 %copy-start.43 = (f32[2048,6]{0,1:T(8,128)}, f32[2048,6]{0,1:T(8,128)S(1)}, u32[]{:S(2)}) copy-start(f32[2048,6]{0,1:T(8,128)S(1)} %get-tuple-element.133) | copy-start | bytes 147460
  24.1 5.1 copy-start.1
  24.1 5.1 copy-start.84
  24.1 5.0 copy-start.86
  24.1 5.0 copy-start.88
  24.2 5.0 copy-start.90
  24.3 14.8 %copy-start.56 = (f32[2048]{0:T(1024)}, f32[2048]{0:T(1024)S(1)}, u32[]{:S(2)}) copy-start(f32[2048]{0:T(1024)S(1)} %get-tuple-element.124) | copy-start | bytes 24580
  24.3 14.8 %copy-start.58 = (f32[2048]{0:T(1024)}, f32[2048]{0:T(1024)S(1)}, u32[]{:S(2)}) copy-start(f32[2048]{0:T(1024)S(1)} %get-tuple-element.125) | copy-start | bytes 24580
  24.3 14.8 %copy-start.60 = (f32[2048]{0:T(1024)}, f32[2048]{0:T(1024)S(1)}, u32[]{:S(2)}) copy-start(f32[2048]{0:T(1024)S(1)} %get-tuple-element.126) | copy-start | bytes 24580
  32.8 5.2 copy-start.4
  32.8 5.2 copy-start.35
  46.5 5.2 copy-start.78
  46.5 5.2 copy-start.95
  46.5 5.5 copy-start.81
  46.5 5.5 copy-start.92
  46.5 5.6 copy-start.102
  48.2 5.3 copy-start.29
  52.9 5.9 copy-start.18
  52.9 63.1 %copy-start.71 = (f32[8,6,256]{2,1,0:T(8,128)}, f32[8,6,256]{2,1,0:T(8,128)S(1)}, u32[]{:S(2)}) copy-start(f32[8,6,256]{2,1,0:T(8,128)S(1)} %copy.190) | copy-start | bytes 147460
  53.5 5.3 copy-start.52
  67.4 31.7 %copy-start.98 = (f32[384]{0:T(512)}, f32[384]{0:T(512)S(1)}, u32[]{:S(2)}) copy-start(f32[384]{0:T(512)S(1)} %mul.880) | copy-start | bytes 4612
  67.4 18.4 %copy-start.68 = (f32[384]{0:T(512)S(1)}, f32[384]{0:T(512)}, u32[]{:S(2)}) copy-start(f32[384]{0:T(512)} %param.34) | copy-start | bytes 4612
  85.8 7.4 %copy-start.66 = (f32[2048]{0:T(1024)}, f32[2048]{0:T(1024)S(1)}, u32[]{:S(2)}) copy-start(f32[2048]{0:T(1024)S(1)} %fusion.72) | copy-start | bytes 24580
  116.1 9.8 %copy-start.42 = (bf16[8,6,128,64]{2,3,1,0:T(8,128)(2,1)S(1)}, bf16[8,6,128,64]{2,3,1,0:T(8,128)(2,1)}, u32[]{:S(2)}) copy-start(bf16[8,6,128,64]{2,3,1,0:T(8,128)(2,1)} %copy-done.41) | copy-start | bytes 2359300
  125.9 5.6 copy-start.79
  125.9 5.6 copy-start.82
  125.9 5.6 copy-start.93
  125.9 5.6 copy-start.96
  125.9 5.6 copy-start.100
  125.9 5.6 copy-start.103
  125.9 5.6 copy-start.114
  131.5 8.6 %copy-start.15 = (f32[8,6,128,64]{2,3,1,0:T(8,128)}, f32[8,6,128,64]{2,3,1,0:T(8,128)S(1)}, u32[]{:S(2)}) copy-start(f32[8,6,128,64]{2,3,1,0:T(8,128)S(1)} %fusion.41) | copy-start | bytes 4718596
  140.1 5.3 copy-start.31
  179.5 6.5 copy-start.2
  179.5 6.5 copy-start.57
  179.5 6.5 copy-start.59
  179.5 6.5 copy-start.61
  201.3 310.0 %all-gather.3.cloned.1.call-start = ((), (), s32[]{:S(2)}) async-start(), calls=%async_computation | async-start | bytes 31457280 | tf_op jit(solution)/shard_map/all_gather | solution.py:161
  208.1 467.8 %all-reduce.24.cloned.1.call-start = ((), (), s32[]{:S(2)}) async-start(), calls=%async_computation.1 | async-start | bytes 8650752 | tf_op jit(solution)/shard_map/psum | solution.py:305
  208.1 5.4 copy-start.5
  208.1 5.4 copy-start.13
  208.2 8.2 %copy-start.17 = (bf16[2048,768]{1,0:T(8,128)(2,1)S(1)}, bf16[2048,768]{1,0:T(8,128)(2,1)}, u32[]{:S(2)}) copy-start(bf16[2048,768]{1,0:T(8,128)(2,1)} %param.19) | copy-start | bytes 9437188
  372.7 9.0 %copy-start.122 = (f32[384]{0:T(512)S(1)}, f32[384]{0:T(512)}, u32[]{:S(2)}) copy-start(f32[384]{0:T(512)} %get-tuple-element.21) | copy-start | bytes 4612
  511.3 12.9 %copy-start.77 = (f32[2048]{0:T(1024)S(1)}, f32[2048]{0:T(1024)}, u32[]{:S(2)}) copy-start(f32[2048]{0:T(1024)} %get-tuple-element.118) | copy-start | bytes 24580
  (84 other events, 224.9 us)
Sparse Core Ops, SparseCore 0:
  201.4 153.2 all-reduce.25
  356.3 154.9 all-gather.2
  516.4 159.4 all-reduce.23
